TPU v7x, 32 devices: a whole 2x2x4 slice. The times are simulated.
32 devices in a mesh: row: 8 (over z, y), col: 4 (over x, core).
Axes of the slice: x: 2, y: 2, z: 4, core: 2. Of those that a mesh axis runs over, the one named last changes fastest.
Arguments:
- orbitals: bfloat16 [20480, 384], P(('row', 'col')), may hold values from -6 to 6
- coulomb: float32 [20480, 20480], P('row', 'col'), may hold values from -0.001953125 to 0.001953125
- interp: bfloat16 [4096, 20480], P('row', 'col'), may hold values from -0.0390625 to 0.0390625
Outputs:
- exchanged: bfloat16 [4096, 384], P(('row', 'col'))
All inputs are finite; a program needn't handle non-finite values.
Results may differ from a plain program's by a relative error of at most 0.018.
Values may be sent and summed in bfloat16 or wider, within the bound.
No kernel may reach another device: no remote copies, remote signals or barrier semaphores. Data moves between devices by JAX's collectives and lax.ppermute only.
A program may use at most 128 MiB of HBM per device.

v0:
```python
import jax
import jax.numpy as jnp
from jax import lax
from jax.sharding import PartitionSpec as P


def broadcast(value, axis, source):
    kept = jnp.where(lax.axis_index(axis) == source, value, 0).astype(value.dtype)
    return lax.psum(kept, axis)


def local(orbitals, coulomb, interp):
    near = lax.all_gather(orbitals, "col", axis=0, tiled=True)
    factor = lax.axis_size("row") // lax.axis_size("col")
    column = lax.axis_index("col")
    pieces = []
    for offset in range(factor):
        pieces.append(broadcast(near, "row", column * factor + offset))
    far = jnp.concatenate(pieces, 0)
    density = lax.dot_general(
        near, far, (((1,), (1,)), ((), ())), preferred_element_type=jnp.float32
    )
    weighted = (coulomb * density).astype(jnp.bfloat16)
    partial_sum = lax.dot_general(
        weighted, near, (((0,), (0,)), ((), ())), preferred_element_type=jnp.float32
    )
    share = lax.psum_scatter(partial_sum, "row", scatter_dimension=0, tiled=True).astype(
        jnp.bfloat16
    )
    contracted = lax.all_gather(share, "row", axis=0, tiled=True)
    terms = jnp.dot(interp, contracted, preferred_element_type=jnp.float32)
    return lax.psum_scatter(terms.astype(jnp.bfloat16), "col", scatter_dimension=0, tiled=True)


def solution(mesh):
    in_specs = (P(("row", "col"), None), P("row", "col"), P("row", "col"))
    out_specs = P(("row", "col"), None)
    return jax.shard_map(local, mesh=mesh, in_specs=in_specs, out_specs=out_specs, check_vma=False)
```

profile of v0, /device:TPU:0, one launch (start us, length us, event | category | flops | bytes accessed | tf_op | source)
XLA Modules:
  0.0 489.1 jit_solution(2194609867817106554)
XLA Ops:
  6.5 0.0 all-gather.3.cloned.1.call-start
  6.5 0.7 all-gather.3.cloned.1.call-update
  7.3 0.0 all-reduce.3.cloned.1.call-start
  7.3 26.2 %all-gather.3.cloned.1.call-done = bf16[2560,384]{1,0:T(8,128)(2,1)} async-done(((bf16[640,384]{1,0:T(8,128)(2,1)}), bf16[2560,384]{1,0:T(8,128)(2,1)}) %all-gather.3.cloned.1.call-update) | async-done | bytes 1966096 | tf_op jit(solution)/shard_map/all_gather | solution.py:13
  33.5 0.0 copy-start
  33.5 4.0 broadcast_select_fusion.1
  37.5 0.0 all-reduce.3.cloned.1.call-update
  37.5 0.0 reduce-scatter.5.cloned.1.call-start
  37.5 149.6 %all-reduce.3.cloned.1.call-done = (bf16[2560,384]{1,0:T(8,128)(2,1)}, bf16[2560,384]{1,0:T(8,128)(2,1)}) async-done(((bf16[2560,384]{1,0:T(8,128)(2,1)}, bf16[2560,384]{1,0:T(8,128)(2,1)}), (bf16[2560,384]{1,0:T(8,128)(2,1)}, bf16[2560,384]{1,0:T(8,128)(2,1)})) %all-reduce.3.cloned.1.call-update) | async-done | bytes 3932176 | tf_op jit(solution)/shard_map/psum | solution.py:9
  187.1 0.0 copy-done
  187.1 58.8 %fusion.1 = f32[5120,384]{1,0:T(8,128)} fusion(bf16[2560,384]{1,0:T(8,128)(2,1)S(1)} %copy-done, f32[2560,5120]{1,0:T(8,128)} %param.4, bf16[2560,384]{1,0:T(8,128)(2,1)} %get-tuple-element.5, bf16[2560,384]{1,0:T(8,128)(2,1)} %get-tuple-element.6), kind=kOutput, calls=%fused_computation.2 | convolution fusion | flops 20166737920 | bytes 66191360 | tf_op jit(solution)/shard_map/dot_general | solution.py:24
  245.9 0.0 reduce-scatter.5.cloned.1.call-update
  246.0 0.0 all-gather.5.cloned.1.call-start
  246.0 139.4 %reduce-scatter.5.cloned.1.call-done = f32[640,384]{1,0:T(8,128)} async-done(((f32[5120,384]{1,0:T(8,128)}), f32[640,384]{1,0:T(8,128)}) %reduce-scatter.5.cloned.1.call-update) | async-done | bytes 983056 | tf_op jit(solution)/shard_map/reduce_scatter | solution.py:27
  385.4 2.0 convert_element_type.16
  387.4 0.0 all-gather.5.cloned.1.call-update
  387.4 0.2 reduce-scatter.7.cloned.1.call-start
  387.7 68.5 %all-gather.5.cloned.1.call-done = bf16[5120,384]{1,0:T(8,128)(2,1)} async-done(((bf16[640,384]{1,0:T(8,128)(2,1)}), bf16[5120,384]{1,0:T(8,128)(2,1)}) %all-gather.5.cloned.1.call-update) | async-done | bytes 3932176 | tf_op jit(solution)/shard_map/all_gather | solution.py:30
  456.2 5.9 %fusion.8 = bf16[512,384]{0,1:T(8,128)(2,1)S(1)} fusion(bf16[5120,384]{1,0:T(8,128)(2,1)} %all-gather.5.cloned.1.call-done, bf16[512,5120]{1,0:T(8,128)(2,1)} %param.5), kind=kOutput, calls=%fused_computation.9 | convolution fusion | flops 2013462528 | bytes 9568256 | tf_op jit(solution)/shard_map/dot_general | solution.py:31
  462.1 0.9 copy.6
  463.0 0.0 reduce-scatter.7.cloned.1.call-update
  463.0 19.6 %reduce-scatter.7.cloned.1.call-done = bf16[128,384]{1,0:T(8,128)(2,1)} async-done(((bf16[512,384]{1,0:T(8,128)(2,1)}), bf16[128,384]{1,0:T(8,128)(2,1)}) %reduce-scatter.7.cloned.1.call-update) | async-done | bytes 98320 | tf_op jit(solution)/shard_map/reduce_scatter | solution.py:32
Async XLA Ops:
  6.5 26.9 %all-gather.3.cloned.1.call-start = ((), (), s32[]{:S(2)}) async-start(), calls=%async_computation.2 | async-start | bytes 2457600 | tf_op jit(solution)/shard_map/all_gather | solution.py:13
  7.3 179.8 %all-reduce.3.cloned.1.call-start = ((), (), s32[]{:S(2)}) async-start(), calls=%async_computation.6 | async-start | bytes 7864320 | tf_op jit(solution)/shard_map/psum | solution.py:9
  33.5 153.6 %copy-start = (bf16[2560,384]{1,0:T(8,128)(2,1)S(1)}, bf16[2560,384]{1,0:T(8,128)(2,1)}, u32[]{:S(2)}) copy-start(bf16[2560,384]{1,0:T(8,128)(2,1)} %all-gather.3.cloned.1.call-done) | copy-start | bytes 5898244
  37.5 347.9 %reduce-scatter.5.cloned.1.call-start = ((), (), s32[]{:S(2)}) async-start(), calls=%async_computation.3 | async-start | bytes 8847360 | tf_op jit(solution)/shard_map/reduce_scatter | solution.py:27
  246.0 210.2 %all-gather.5.cloned.1.call-start = ((), (), s32[]{:S(2)}) async-start(), calls=%async_computation.4 | async-start | bytes 4423680 | tf_op jit(solution)/shard_map/all_gather | solution.py:30
  387.4 95.2 %reduce-scatter.7.cloned.1.call-start = ((), (), s32[]{:S(2)}) async-start(), calls=%async_computation.5 | async-start | bytes 491520 | tf_op jit(solution)/shard_map/reduce_scatter | solution.py:32
Sparse Core Ops, SparseCore 0:
  8.9 24.5 all-gather.2
  37.6 149.4 all-reduce.2
  246.1 139.2 reduce-scatter.4
  387.5 68.5 all-gather.4
  463.2 19.4 reduce-scatter.6
where the time goes:
time: 489 us
  waiting for transfers between devices  404 us (83%)
  matrix products  64.8 us (13%)
  between operations  13.2 us (3%)
  other arithmetic  6.01 us (1%)
    psum x1, waiting for transfers between devices, broadcast(): return lax.psum(kept, axis)  150 us
    reduce_scatter x1, waiting for transfers between devices, local(): lax.psum_scatter(partial_sum, 'row', scatter_dimension=0, tiled=True)  139 us
    all_gather x1, waiting for transfers between devices, local(): contracted = lax.all_gather(share, 'row', axis=0, tiled=True)  68.5 us
    dot_general x1, matrix products, local(): lax.dot_general(weighted, near, (((0,), (0,)), ((), ())), preferred_eleme...  58.8 us
    all_gather x1, waiting for transfers between devices, local(): near = lax.all_gather(orbitals, 'col', axis=0, tiled=True)  26.2 us
    reduce_scatter x1, waiting for transfers between devices, local(): lax.psum_scatter(terms.astype(jnp.bfloat16), 'col', scatter_dimension=0,...  19.6 us
  transfers between devices with their start and end apart: 5, of which 5 were waited for; matrix products, arithmetic and copies ran while one was open for 0% of the time, Pallas kernels for 0%

commit v1 on v0

--- a/solution.py
+++ b/solution.py
@@ -6,7 +6,11 @@
 
 def broadcast(value, axis, source):
     kept = jnp.where(lax.axis_index(axis) == source, value, 0).astype(value.dtype)
-    return lax.psum(kept, axis)
+
+    def compute_zones(load):
+        return jnp.sum(lax.all_gather(load, axis_name=axis), axis=0)
+
+    return compute_zones(kept)
 
 
 def local(orbitals, coulomb, interp):

time: 489 us -> 779 us (1.59)
  waiting for transfers between devices: 404 us -> 673 us
  other arithmetic: 6.01 us -> 26.4 us
    all_gather x0 -> x2, waiting for transfers between devices: none -> 418 us  [compute_zones(): return jnp.sum(lax.all_gather(load, axis_name=axis), axis=0)]
    psum x1 -> x0, waiting for transfers between devices: 150 us -> none  [broadcast(): return lax.psum(kept, axis)]
    reduce_sum x0 -> x2, other arithmetic: none -> 20.5 us  [compute_zones(): return jnp.sum(lax.all_gather(load, axis_name=axis), axis=0)]
  transfers between devices with their start and end apart: 5 -> 6, of which waited for: 5 -> 6; matrix products, arithmetic and copies ran while one was open for 0% -> 1% of each run, Pallas kernels for 0% -> 0%
where the time goes in v1:
time: 779 us; the launch traced here: 778 us
  waiting for transfers between devices  673 us (86%)
  matrix products  64.7 us (8%)
  other arithmetic  26.4 us (3%)
  between operations  13.5 us (2%)
    all_gather x2, waiting for transfers between devices, compute_zones(): return jnp.sum(lax.all_gather(load, axis_name=axis), axis=0)  418 us
    reduce_scatter x1, waiting for transfers between devices, local(): lax.psum_scatter(partial_sum, 'row', scatter_dimension=0, tiled=True)  138 us
    all_gather x1, waiting for transfers between devices, local(): contracted = lax.all_gather(share, 'row', axis=0, tiled=True)  68.4 us
    dot_general x1, matrix products, local(): lax.dot_general(weighted, near, (((0,), (0,)), ((), ())), preferred_eleme...  58.8 us
    all_gather x1, waiting for transfers between devices, local(): near = lax.all_gather(orbitals, 'col', axis=0, tiled=True)  26.2 us
    reduce_sum x2, other arithmetic, compute_zones(): return jnp.sum(lax.all_gather(load, axis_name=axis), axis=0)  20.5 us
    reduce_scatter x1, waiting for transfers between devices, local(): lax.psum_scatter(terms.astype(jnp.bfloat16), 'col', scatter_dimension=0,...  19.6 us
  transfers between devices with their start and end apart: 6, of which 6 were waited for; matrix products, arithmetic and copies ran while one was open for 1% of the time, Pallas kernels for 0%

profile of v1, /device:TPU:0, one launch (start us, length us, event | category | flops | bytes accessed | tf_op | source)
XLA Modules:
  0.0 778.4 jit_solution(4564824747678490580)
XLA Ops:
  6.5 0.0 all-gather.7.cloned.1.call-start
  6.5 0.7 all-gather.7.cloned.1.call-update
  7.3 0.0 all-gather.11.cloned.1.call-start
  7.3 26.2 %all-gather.7.cloned.1.call-done = bf16[2560,384]{1,0:T(8,128)(2,1)} async-done(((bf16[640,384]{1,0:T(8,128)(2,1)}), bf16[2560,384]{1,0:T(8,128)(2,1)}) %all-gather.7.cloned.1.call-update) | async-done | bytes 1966096 | tf_op jit(solution)/shard_map/all_gather | solution.py:17
  33.5 3.8 broadcast_select_fusion.1
  37.3 0.0 all-gather.11.cloned.1.call-update
  37.3 0.0 all-gather.13.cloned.1.call-start
  37.4 0.7 all-gather.13.cloned.1.call-update
  38.1 0.0 reduce-scatter.5.cloned.1.call-start
  38.1 213.8 %all-gather.11.cloned.1.call-done = bf16[20480,384]{1,0:T(8,128)(2,1)} async-done(((bf16[2560,384]{1,0:T(8,128)(2,1)}), bf16[20480,384]{1,0:T(8,128)(2,1)}) %all-gather.11.cloned.1.call-update) | async-done | bytes 15728656 | tf_op jit(solution)/shard_map/all_gather | solution.py:11
  251.9 10.3 %reduce_sum.24 = bf16[2560,384]{1,0:T(8,128)(2,1)} reduce(bf16[8,2560,384]{2,1,0:T(8,128)(2,1)} %bitcast.15, bf16[]{:T(256)} %constant.17.clone.1), dimensions={0}, to_apply=%region_0.1 | reduce | flops 6881280 | bytes 17694722 | tf_op jit(solution)/shard_map/reduce_sum | solution.py:11
  262.3 204.5 %all-gather.13.cloned.1.call-done = bf16[20480,384]{1,0:T(8,128)(2,1)} async-done(((bf16[2560,384]{1,0:T(8,128)(2,1)}), bf16[20480,384]{1,0:T(8,128)(2,1)}) %all-gather.13.cloned.1.call-update) | async-done | bytes 15728656 | tf_op jit(solution)/shard_map/all_gather | solution.py:11
  466.8 0.0 copy-start
  466.8 10.2 %reduce_sum.25 = bf16[2560,384]{1,0:T(8,128)(2,1)} reduce(bf16[8,2560,384]{2,1,0:T(8,128)(2,1)} %bitcast.16, bf16[]{:T(256)} %constant.17.clone.1), dimensions={0}, to_apply=%region_1.2 | reduce | flops 6881280 | bytes 17694722 | tf_op jit(solution)/shard_map/reduce_sum | solution.py:11
  477.0 0.0 copy-done
  477.0 58.8 %fusion.1 = f32[5120,384]{1,0:T(8,128)} fusion(bf16[2560,384]{1,0:T(8,128)(2,1)S(1)} %copy-done, f32[2560,5120]{1,0:T(8,128)} %param.4, bf16[2560,384]{1,0:T(8,128)(2,1)} %reduce_sum.25, bf16[2560,384]{1,0:T(8,128)(2,1)} %reduce_sum.24), kind=kOutput, calls=%fused_computation.2 | convolution fusion | flops 20166737920 | bytes 66191360 | tf_op jit(solution)/shard_map/dot_general | solution.py:28
  535.8 0.0 reduce-scatter.5.cloned.1.call-update
  535.8 0.0 all-gather.9.cloned.1.call-start
  535.9 138.5 %reduce-scatter.5.cloned.1.call-done = f32[640,384]{1,0:T(8,128)} async-done(((f32[5120,384]{1,0:T(8,128)}), f32[640,384]{1,0:T(8,128)}) %reduce-scatter.5.cloned.1.call-update) | async-done | bytes 983056 | tf_op jit(solution)/shard_map/reduce_scatter | solution.py:31
  674.4 2.0 convert_element_type.20
  676.4 0.0 all-gather.9.cloned.1.call-update
  676.4 0.3 reduce-scatter.7.cloned.1.call-start
  676.7 68.4 %all-gather.9.cloned.1.call-done = bf16[5120,384]{1,0:T(8,128)(2,1)} async-done(((bf16[640,384]{1,0:T(8,128)(2,1)}), bf16[5120,384]{1,0:T(8,128)(2,1)}) %all-gather.9.cloned.1.call-update) | async-done | bytes 3932176 | tf_op jit(solution)/shard_map/all_gather | solution.py:34
  745.2 5.9 fusion.8
  751.1 0.9 copy.6
  752.0 0.0 reduce-scatter.7.cloned.1.call-update
  752.0 19.6 %reduce-scatter.7.cloned.1.call-done = bf16[128,384]{1,0:T(8,128)(2,1)} async-done(((bf16[512,384]{1,0:T(8,128)(2,1)}), bf16[128,384]{1,0:T(8,128)(2,1)}) %reduce-scatter.7.cloned.1.call-update) | async-done | bytes 98320 | tf_op jit(solution)/shard_map/reduce_scatter | solution.py:36
Async XLA Ops:
  6.5 26.9 %all-gather.7.cloned.1.call-start = ((), (), s32[]{:S(2)}) async-start(), calls=%async_computation.2 | async-start | bytes 2457600 | tf_op jit(solution)/shard_map/all_gather | solution.py:17
  7.3 244.7 %all-gather.11.cloned.1.call-start = ((), (), s32[]{:S(2)}) async-start(), calls=%async_computation.5 | async-start | bytes 17694720 | tf_op jit(solution)/shard_map/all_gather | solution.py:11
  37.3 429.5 %all-gather.13.cloned.1.call-start = ((), (), s32[]{:S(2)}) async-start(), calls=%async_computation.6 | async-start | bytes 17694720 | tf_op jit(solution)/shard_map/all_gather | solution.py:11
  38.1 636.3 %reduce-scatter.5.cloned.1.call-start = ((), (), s32[]{:S(2)}) async-start(), calls=%async_computation.3 | async-start | bytes 8847360 | tf_op jit(solution)/shard_map/reduce_scatter | solution.py:31
  466.8 10.2 %copy-start = (bf16[2560,384]{1,0:T(8,128)(2,1)S(1)}, bf16[2560,384]{1,0:T(8,128)(2,1)}, u32[]{:S(2)}) copy-start(bf16[2560,384]{1,0:T(8,128)(2,1)} %all-gather.7.cloned.1.call-done) | copy-start | bytes 5898244
  535.8 209.3 %all-gather.9.cloned.1.call-start = ((), (), s32[]{:S(2)}) async-start(), calls=%async_computation.4 | async-start | bytes 4423680 | tf_op jit(solution)/shard_map/all_gather | solution.py:34
  676.4 95.2 %reduce-scatter.7.cloned.1.call-start = ((), (), s32[]{:S(2)}) async-start(), calls=%async_computation.7 | async-start | bytes 491520 | tf_op jit(solution)/shard_map/reduce_scatter | solution.py:36
Sparse Core Ops, SparseCore 0:
  8.9 24.5 all-gather.6
  37.4 214.4 all-gather.10
  254.1 212.6 all-gather.12
  536.0 138.3 reduce-scatter.4
  676.6 68.5 all-gather.8
  752.1 19.4 reduce-scatter.6
